TPU v7x, 512 devices: a whole 4x8x8 slice. The times are simulated.
512 devices in a mesh: doc: 32 (over y, x), seq: 16 (over z, core).
Axes of the slice: x: 4, y: 8, z: 8, core: 2. Of those that a mesh axis runs over, the one named last changes fastest.
Arguments:
- tokens: bfloat16 [131072, 1024], P(('doc', 'seq')), parts along dimension 0, may hold values from -8 to 8
- bottom_qkv: bfloat16 [1024, 3072], P('seq'), may hold values from -1 to 1
- bottom_out: bfloat16 [1024, 1024], P('seq'), may hold values from -0.5 to 0.5
- top_qkv: bfloat16 [1024, 3, 1024], P(None, None, 'seq'), may hold values from -1 to 1
- top_out: bfloat16 [1024, 1024], P('seq'), may hold values from -0.5 to 0.5
- cross_query: bfloat16 [1024, 1024], P('seq'), may hold values from -1 to 1
- cross_kv: bfloat16 [1024, 2, 1024], P(None, None, 'seq'), may hold values from -1 to 1
- cross_out: bfloat16 [1024, 1024], P('seq'), may hold values from -0.5 to 0.5
Outputs:
- encoded: bfloat16 [131072, 1024], P(('doc', 'seq')), parts along dimension 0
There are 32 independent parts, one for each index of `doc`. A program takes and returns all parts, laid end to end along the dimension named above; an argument that names none is the same for every part. Nothing has to cross between parts.
All inputs are finite; a program needn't handle non-finite values.
Results may differ from a plain program's by a relative error of at most 0.013.
Values may be sent and summed in bfloat16 or wider, within the bound.
A program may use at most 64 MiB of HBM per device.

v0:
```python
import math
import jax
import jax.numpy as jnp
from jax import lax
from jax.sharding import PartitionSpec as P

H = 16
W = 512
POOL = 32
EPS = 1e-06


def padded(cells, sides, width):
    for axis, dim in sides:
        count = lax.axis_size(axis)
        ends = count - 1
        head = lax.slice_in_dim(cells, 0, width, axis=dim)
        tail = lax.slice_in_dim(cells, cells.shape[dim] - width, cells.shape[dim], axis=dim)
        cells = jnp.concatenate(
            [
                lax.ppermute(tail, axis, [(i, (i + 1) % count) for i in range(ends)]),
                cells,
                lax.ppermute(head, axis, [((i + 1) % count, i) for i in range(ends)]),
            ],
            axis=dim,
        )
    return cells


def normed(values_in):
    values_in = values_in.astype(jnp.float32)
    return (
        values_in * lax.rsqrt(jnp.mean(values_in * values_in, axis=-1, keepdims=True) + EPS)
    ).astype(jnp.bfloat16)


def window_mask(first_tok, tok_count, half_win, total_tok):
    query_pos = first_tok + jnp.arange(tok_count, dtype=jnp.int32)
    key_pos = first_tok - half_win + jnp.arange(tok_count + 2 * half_win, dtype=jnp.int32)
    offsets = key_pos[None, :] - query_pos[:, None]
    inside = (key_pos[None, :] >= 0) & (key_pos[None, :] < total_tok)
    return (offsets >= -half_win) & (offsets < half_win) & inside


def attend(queries, key_mat, value_mat, allowed, head_count):
    row_count = queries.shape[0]
    key_count = key_mat.shape[0]
    head_width = queries.shape[1] // head_count
    score_scale = 1.0 / math.sqrt(head_width)
    split_q = queries.reshape(row_count, head_count, head_width).transpose(1, 0, 2)
    split_k = key_mat.reshape(key_count, head_count, head_width).transpose(1, 0, 2)
    split_v = value_mat.reshape(key_count, head_count, head_width).transpose(1, 0, 2)

    def one_head(operands):
        query_h, key_h, value_h = operands
        scores = jnp.dot(query_h, key_h.T, preferred_element_type=jnp.float32) * score_scale
        if allowed is not None:
            scores = jnp.where(allowed, scores, -1e30)
        row_peak = jnp.max(scores, axis=1, keepdims=True)
        expo = jnp.exp(scores - row_peak)
        row_total = jnp.sum(expo, axis=1, keepdims=True)
        mixture = (
            jnp.dot(expo.astype(jnp.bfloat16), value_h, preferred_element_type=jnp.float32)
            / row_total
        )
        return mixture.astype(jnp.bfloat16)

    merged = lax.map(one_head, (split_q, split_k, split_v))
    return merged.transpose(1, 0, 2).reshape(row_count, head_count * head_width)


def fold_rows(operand, shard_rows):
    return jnp.dot(operand, shard_rows, preferred_element_type=jnp.float32)


def local(tokens, bottom_qkv, bottom_out, top_qkv, top_out, cross_query, cross_kv, cross_out):
    tok_count, model_width = tokens.shape
    devices_seq = lax.axis_size("seq")
    local_heads = H // devices_seq
    half_win = W // 2
    total_tok = tok_count * devices_seq
    first_tok = lax.axis_index("seq") * tok_count
    normed_tok = normed(tokens)
    project = fold_rows(normed_tok, lax.all_gather(bottom_qkv, "seq", axis=0, tiled=True))
    project = project.astype(jnp.bfloat16)
    queries = project[:, :model_width]
    key_vals = padded(project[:, model_width:], (("seq", 0),), half_win)
    allowed = window_mask(first_tok, tok_count, half_win, total_tok)
    attended = attend(queries, key_vals[:, :model_width], key_vals[:, model_width:], allowed, H)
    out_sum = fold_rows(attended, lax.all_gather(bottom_out, "seq", axis=0, tiled=True))
    lower_tok = (tokens.astype(jnp.float32) + out_sum).astype(jnp.bfloat16)
    pooled = jnp.mean(
        lower_tok.astype(jnp.float32).reshape(tok_count // POOL, POOL, model_width), axis=1
    ).astype(jnp.bfloat16)
    all_units = lax.all_gather(pooled, "seq", axis=0, tiled=True)
    unit_norm = normed(all_units)
    top_q = jnp.dot(unit_norm, top_qkv[:, 0, :], preferred_element_type=jnp.float32).astype(
        jnp.bfloat16
    )
    top_k = jnp.dot(unit_norm, top_qkv[:, 1, :], preferred_element_type=jnp.float32).astype(
        jnp.bfloat16
    )
    top_v = jnp.dot(unit_norm, top_qkv[:, 2, :], preferred_element_type=jnp.float32).astype(
        jnp.bfloat16
    )
    top_att = attend(top_q, top_k, top_v, None, local_heads)
    head_term = jnp.dot(top_att, top_out, preferred_element_type=jnp.float32)
    head_total = lax.psum(head_term.astype(jnp.bfloat16), "seq").astype(jnp.float32)
    top_units = (all_units.astype(jnp.float32) + head_total).astype(jnp.bfloat16)
    upper_norm = normed(top_units)
    part_keys = jnp.dot(upper_norm, cross_kv[:, 0, :], preferred_element_type=jnp.float32).astype(
        jnp.bfloat16
    )
    part_vals = jnp.dot(upper_norm, cross_kv[:, 1, :], preferred_element_type=jnp.float32).astype(
        jnp.bfloat16
    )
    stacked = jnp.concatenate([part_keys, part_vals], axis=1)
    gathered = lax.all_gather(stacked, "seq", axis=1, tiled=True)
    unit_count = gathered.shape[0]
    arranged = gathered.reshape(unit_count, devices_seq, 2, part_keys.shape[1])
    cross_keys = arranged[:, :, 0, :].reshape(unit_count, model_width)
    cross_vals = arranged[:, :, 1, :].reshape(unit_count, model_width)
    lower_norm = normed(lower_tok)
    query_acc = fold_rows(lower_norm, lax.all_gather(cross_query, "seq", axis=0, tiled=True))
    cross_q = query_acc.astype(jnp.bfloat16)
    cross_att = attend(cross_q, cross_keys, cross_vals, None, H)
    cross_sum = fold_rows(cross_att, lax.all_gather(cross_out, "seq", axis=0, tiled=True))
    return (lower_tok.astype(jnp.float32) + cross_sum).astype(jnp.bfloat16)


def solution(mesh):
    in_specs = (
        P(("doc", "seq"), None),
        P("seq", None),
        P("seq", None),
        P(None, None, "seq"),
        P("seq", None),
        P("seq", None),
        P(None, None, "seq"),
        P("seq", None),
    )
    out_specs = P(("doc", "seq"), None)
    return jax.shard_map(local, mesh=mesh, in_specs=in_specs, out_specs=out_specs, check_vma=False)
```

profile of v0, /device:TPU:1, one launch (start us, length us, event | category | flops | bytes accessed | tf_op | source)
XLA Modules:
  0.0 322.5 jit_solution(8568578363218023782)
XLA Ops:
  6.5 0.7 all-gather.5.cloned.1.call-update
  7.3 0.7 all-gather.7.cloned.1.call-update
  8.1 1.2 fusion.39
  9.3 55.6 %all-gather.5.cloned.1.call-done = bf16[1024,3072]{1,0:T(8,128)(2,1)} async-done(((bf16[64,3072]{1,0:T(8,128)(2,1)}), bf16[1024,3072]{1,0:T(8,128)(2,1)}) %all-gather.5.cloned.1.call-update) | async-done | bytes 6291472 | tf_op jit(solution)/shard_map/all_gather | solution.py:84
  64.9 4.8 %convolution_convert_fusion = bf16[256,3072]{1,0:T(8,128)(2,1)S(1)} fusion(bf16[1024,3072]{1,0:T(8,128)(2,1)} %all-gather.5.cloned.1.call-done, bf16[256,1024]{1,0:T(8,128)(2,1)} %param.12, f32[256]{0:T(256)S(1)} %add_rsqrt_fusion.1), kind=kOutput, calls=%fused_computation.40 | convolution fusion | flops 1612185600 | bytes 8389632 | tf_op jit(solution)/shard_map/dot_general | solution.py:73
  69.8 2.7 collective-permute-start
  72.5 2.6 collective-permute-start.1
  75.3 1.0 copy.15
  76.3 10.8 %collective-permute-done = bf16[256,2048]{1,0:T(8,128)(2,1)} collective-permute-done((bf16[256,2048]{1,0:T(8,128)(2,1)S(1)}, bf16[256,2048]{1,0:T(8,128)(2,1)}, u32[]{:S(2)}, u32[]{:S(2)}) %collective-permute-start) | collective-permute-done | bytes 1048608 | tf_op jit(solution)/shard_map/ppermute | solution.py:21
  87.1 6.1 %collective-permute-done.1 = bf16[256,2048]{1,0:T(8,128)(2,1)} collective-permute-done((bf16[256,2048]{1,0:T(8,128)(2,1)S(1)}, bf16[256,2048]{1,0:T(8,128)(2,1)}, u32[]{:S(2)}, u32[]{:S(2)}) %collective-permute-start.1) | collective-permute-done | bytes 1048608 | tf_op jit(solution)/shard_map/ppermute | solution.py:23
  93.2 1.7 pad_maximum_fusion
  95.2 1.6 copy.16
  96.8 0.7 copy.17
  97.6 33.1 %while.26 = (s32[]{:T(128)}, bf16[16,256,64]{1,2,0:T(8,128)(2,1)S(1)}, bf16[16,256,64]{1,2,0:T(8,128)(2,1)}, bf16[16,768,64]{1,2,0:T(8,128)(2,1)}, bf16[16,768,6...) while((s32[]{:T(128)}, ...), condition=%wide.region_4.5_spmd.clone, body=%wide.region_1.4_spmd.clone.sunk | while | flops 52723200 | bytes 2633565 | solution.py:68
  97.6 1.4 fusion.111
  99.3 0.4 fusion.113
  99.7 1.4 fusion.111
  101.4 0.4 fusion.113
  101.8 1.4 fusion.111
  103.4 0.4 fusion.113
  103.8 1.4 fusion.111
  105.9 1.4 fusion.111
  108.0 1.4 fusion.111
  110.0 1.4 fusion.111
  112.1 1.4 fusion.111
  114.1 1.4 fusion.111
  116.2 1.4 fusion.111
  118.3 1.4 fusion.111
  120.3 1.4 fusion.111
  122.4 1.4 fusion.111
  124.5 1.4 fusion.111
  126.5 1.4 fusion.111
  128.6 1.4 fusion.111
  130.7 2.4 bitcast_reduce_fusion
  133.1 16.1 %all_gather.21 = bf16[128,1024]{1,0:T(8,128)(2,1)S(1)} all-gather(bf16[8,1024]{1,0:T(8,128)(2,1)S(1)} %multiply_convert_fusion.2), channel_id=1, replica_groups=mesh['doc'=32,'seq'=16] {'seq'}, dimensions={0}, use_global_device_ids=true | all-gather | bytes 278528 | tf_op jit(solution)/shard_map/all_gather | solution.py:95
  149.7 0.4 fusion.80
  150.1 0.4 fusion.38
  150.6 0.9 convolution_convert_fusion.2
  151.6 0.5 all-gather.11.cloned.1.call-update
  152.4 2.3 convolution_convert_fusion.1
  154.9 112.5 %all-reduce.2.cloned.1.call-done = bf16[128,1024]{1,0:T(8,128)(2,1)} async-done(((bf16[128,1024]{1,0:T(8,128)(2,1)}), bf16[128,1024]{1,0:T(8,128)(2,1)}) %all-reduce.2.cloned.1.call-update) | async-done | bytes 262160 | tf_op jit(solution)/shard_map/psum | solution.py:108
  267.4 1.1 fusion.41
  268.6 1.2 convolution_convert_fusion.7
  269.8 1.2 convolution_convert_fusion.6
  271.1 16.9 %all_gather.22 = bf16[128,2048]{0,1:T(8,128)(2,1)S(1)} all-gather(bf16[128,128]{0,1:T(8,128)(2,1)S(1)} %pad_maximum_fusion.1), channel_id=1, replica_groups=mesh['doc'=32,'seq'=16] {'seq'}, dimensions={1}, use_global_device_ids=true | all-gather | bytes 557056 | tf_op jit(solution)/shard_map/all_gather | solution.py:118
  288.7 7.1 %while.25 = (s32[]{:T(128)}, bf16[16,256,64]{1,2,0:T(8,128)(2,1)S(1)}, bf16[16,256,64]{1,2,0:T(8,128)(2,1)S(1)}, bf16[16,128,64]{2,1,0:T(8,128)(2,1)S(1)}, bf16[16,128,64]{2,1,0:T(8,128)(2,1)S(1)}, /*index=5*/s32[]{:T(128)}) while((s32[]{:T(128)}, bf16[16,256,64]{1,2,0:T(8,128)(2,1)S(1)}, bf16[16,256,64]{1,2,0:T(8,128)(2,1)S(1)}, ...), condition=%wide.region_15.16_spmd, body=%wide.region_12.15_spmd.sunk | while | flops 8617474 | bytes 531525 | solution.py:68
  295.8 17.0 %all-gather.11.cloned.1.call-done = bf16[1024,1024]{1,0:T(8,128)(2,1)} async-done(((bf16[64,1024]{1,0:T(8,128)(2,1)}), bf16[1024,1024]{1,0:T(8,128)(2,1)}) %all-gather.11.cloned.1.call-update) | async-done | bytes 2097168 | tf_op jit(solution)/shard_map/all_gather | solution.py:127
  312.8 3.1 fusion.37
  (116 shorter events, 18.5 us)
Async XLA Ops:
  6.5 144.0 %copy-start = (bf16[64,1024]{1,0:T(8,128)(2,1)S(1)}, bf16[64,1024]{1,0:T(8,128)(2,1)}, u32[]{:S(2)}) copy-start(bf16[64,1024]{1,0:T(8,128)(2,1)} %param.16) | copy-start | bytes 393220
  6.5 58.4 %all-gather.5.cloned.1.call-start = ((), (), s32[]{:S(2)}) async-start(), calls=%async_computation | async-start | bytes 6684672 | tf_op jit(solution)/shard_map/all_gather | solution.py:84
  7.3 123.4 %all-gather.7.cloned.1.call-start = ((), (), s32[]{:S(2)}) async-start(), calls=%async_computation.1 | async-start | bytes 2228224 | tf_op jit(solution)/shard_map/all_gather | solution.py:90
  8.0 144.4 %all-gather.9.cloned.1.call-start = ((), (), s32[]{:S(2)}) async-start(), calls=%async_computation.2 | async-start | bytes 2228224 | tf_op jit(solution)/shard_map/all_gather | solution.py:124
  69.8 17.2 %collective-permute-start = (bf16[256,2048]{1,0:T(8,128)(2,1)S(1)}, bf16[256,2048]{1,0:T(8,128)(2,1)}, u32[]{:S(2)}, u32[]{:S(2)}) collective-permute-start(bf16[256,2048]{1,0:T(8,128)(2,1)S(1)} %slice.45), channel_id=1, source_target_pairs={{0,1},{1,2},{2,3},{3,4},{4,5},{5,6},{6,7},{7,8},{8,9},{9,10},{10,1... | collective-permute-start | bytes 3145736 | tf_op jit(solution)/shard_map/ppermute | solution.py:21
  72.5 20.7 %collective-permute-start.1 = (bf16[256,2048]{1,0:T(8,128)(2,1)S(1)}, bf16[256,2048]{1,0:T(8,128)(2,1)}, u32[]{:S(2)}, u32[]{:S(2)}) collective-permute-start(bf16[256,2048]{1,0:T(8,128)(2,1)S(1)} %slice.45), channel_id=1, source_target_pairs={{1,0},{2,1},{3,2},{4,3},{5,4},{6,5},{7,6},{8,7},{9,8},{10,9},{11,1... | collective-permute-start | bytes 3145736 | tf_op jit(solution)/shard_map/ppermute | solution.py:23
  75.2 192.3 %all-reduce.2.cloned.1.call-start = ((), (), s32[]{:S(2)}) async-start(), calls=%async_computation.3 | async-start | bytes 524288 | tf_op jit(solution)/shard_map/psum | solution.py:108
  97.6 33.1 %copy-start.1 = (bf16[256,1024]{1,0:T(8,128)(2,1)S(1)}, bf16[256,1024]{1,0:T(8,128)(2,1)}, u32[]{:S(2)}) copy-start(bf16[256,1024]{1,0:T(8,128)(2,1)} %param.12) | copy-start | bytes 1572868
  130.7 18.7 %copy-start.2 = (bf16[1024,3,64]{0,2,1:T(8,128)(2,1)S(1)}, bf16[1024,3,64]{0,2,1:T(8,128)(2,1)}, u32[]{:S(2)}) copy-start(bf16[1024,3,64]{0,2,1:T(8,128)(2,1)} %param.15) | copy-start | bytes 1179652
  151.5 161.3 %all-gather.11.cloned.1.call-start = ((), (), s32[]{:S(2)}) async-start(), calls=%async_computation.4 | async-start | bytes 2228224 | tf_op jit(solution)/shard_map/all_gather | solution.py:127
  152.3 116.3 %copy-start.3 = (bf16[1024,2,64]{0,2,1:T(8,128)(2,1)S(1)}, bf16[1024,2,64]{0,2,1:T(8,128)(2,1)}, u32[]{:S(2)}) copy-start(bf16[1024,2,64]{0,2,1:T(8,128)(2,1)} %param.18) | copy-start | bytes 786436
Sparse Core Ops, SparseCore 0:
  9.5 55.3 all-gather.4
  67.0 41.1 all-gather.6
  110.3 42.0 all-gather.8
  154.6 112.8 all-reduce.1
  269.6 43.1 all-gather.10
where the time goes:
time: 323 us; the launch traced here: 322 us
  waiting for transfers between devices  204 us (63%)
  matrix products  51.4 us (16%)
  blocking collectives  33 us (10%)
  between operations  13.4 us (4%)
  other arithmetic  9.66 us (3%)
  starting transfers between devices  5.46 us (2%)
  local copies, waits for them, and re-layouts  4.62 us (1%)
    psum x1, waiting for transfers between devices, local(): lax.psum(head_term.astype(jnp.bfloat16), 'seq').astype(jnp.float32)  113 us
    all_gather x1, waiting for transfers between devices, local(): lax.all_gather(bottom_qkv, 'seq', axis=0, tiled=True)  55.6 us
    dot_general x33, matrix products, one_head(): jnp.dot(query_h, key_h.T, preferred_element_type=jnp.float32) * score_scale  25.3 us
    all_gather x1, waiting for transfers between devices, local(): lax.all_gather(cross_out, 'seq', axis=0, tiled=True)  17 us
    all_gather x1, blocking collectives, local(): gathered = lax.all_gather(stacked, 'seq', axis=1, tiled=True)  16.9 us
    all_gather x1, blocking collectives, local(): all_units = lax.all_gather(pooled, 'seq', axis=0, tiled=True)  16.1 us
    dot_general x4, matrix products, fold_rows(): return jnp.dot(operand, shard_rows, preferred_element_type=jnp.float32)  12.7 us
    ppermute x1, waiting for transfers between devices, padded(): lax.ppermute(tail, axis, [(i, (i + 1) % count) for i in range(ends)])  10.8 us
  transfers between devices with their start and end apart: 7, of which 6 were waited for; matrix products, arithmetic and copies ran while one was open for 19% of the time, Pallas kernels for 0%

commit v1 on v0

--- a/solution.py
+++ b/solution.py
@@ -81,7 +81,12 @@
     total_tok = tok_count * devices_seq
     first_tok = lax.axis_index("seq") * tok_count
     normed_tok = normed(tokens)
-    project = fold_rows(normed_tok, lax.all_gather(bottom_qkv, "seq", axis=0, tiled=True))
+    project = fold_rows(
+        normed_tok,
+        jnp.concatenate(
+            lax.all_to_all(jnp.stack([bottom_qkv] * lax.axis_size("seq")), "seq", 0, 0), axis=0
+        ),
+    )
     project = project.astype(jnp.bfloat16)
     queries = project[:, :model_width]
     key_vals = padded(project[:, model_width:], (("seq", 0),), half_win)

time: 323 us -> 439 us (1.36)
  waiting for transfers between devices: 204 us -> 289 us
  matrix products: 51.4 us -> 65.4 us
  starting transfers between devices: 5.46 us -> 17.4 us
  local copies, waits for them, and re-layouts: 4.62 us -> 9.99 us
    all_to_all x0 -> x1, waiting for transfers between devices: none -> 147 us  [local(): lax.all_to_all(jnp.stack([bottom_qkv] * lax.axis_size('seq')), 'seq', 0, 0)]
    all_gather x1 -> x0, waiting for transfers between devices: 55.6 us -> none  [local(): lax.all_gather(bottom_qkv, 'seq', axis=0, tiled=True)]
    dot_general x33, matrix products: 9.71 us -> 24 us  [one_head(): jnp.dot(expo.astype(jnp.bfloat16), value_h, preferred_element_type=jnp.fl...]
    all_to_all x0 -> x1, starting transfers between devices: none -> 12 us  [local(): lax.all_to_all(jnp.stack([bottom_qkv] * lax.axis_size('seq')), 'seq', 0, 0)]
    another operation x2 -> x3, local copies, waits for them, and re-layouts: 0.1 us -> 4.58 us  [the longest x1 4.49 us: local(): jnp.stack([bottom_qkv] * lax.axis_size('seq'))]
  transfers between devices with their start and end apart: 7 -> 7, of which waited for: 6 -> 5; matrix products, arithmetic and copies ran while one was open for 19% -> 17% of each run, Pallas kernels for 0% -> 0%
where the time goes in v1:
time: 439 us; the launch traced here: 438 us
  waiting for transfers between devices  289 us (66%)
  matrix products  65.4 us (15%)
  blocking collectives  33.4 us (8%)
  starting transfers between devices  17.4 us (4%)
  between operations  13.4 us (3%)
  local copies, waits for them, and re-layouts  9.99 us (2%)
  other arithmetic  8.6 us (2%)
    all_to_all x1, waiting for transfers between devices, local(): lax.all_to_all(jnp.stack([bottom_qkv] * lax.axis_size('seq')), 'seq', 0, 0)  147 us
    psum x1, waiting for transfers between devices, local(): lax.psum(head_term.astype(jnp.bfloat16), 'seq').astype(jnp.float32)  111 us
    dot_general x33, matrix products, one_head(): jnp.dot(query_h, key_h.T, preferred_element_type=jnp.float32) * score_scale  25.2 us
    dot_general x33, matrix products, one_head(): jnp.dot(expo.astype(jnp.bfloat16), value_h, preferred_element_type=jnp.fl...  24 us
    all_gather x1, waiting for transfers between devices, local(): lax.all_gather(cross_out, 'seq', axis=0, tiled=True)  17.2 us
    all_gather x1, blocking collectives, local(): gathered = lax.all_gather(stacked, 'seq', axis=1, tiled=True)  16.9 us
    all_gather x1, blocking collectives, local(): all_units = lax.all_gather(pooled, 'seq', axis=0, tiled=True)  16.4 us
    dot_general x4, matrix products, fold_rows(): return jnp.dot(operand, shard_rows, preferred_element_type=jnp.float32)  12.5 us
  transfers between devices with their start and end apart: 7, of which 5 were waited for; matrix products, arithmetic and copies ran while one was open for 17% of the time, Pallas kernels for 0%

profile of v1, /device:TPU:1, one launch (start us, length us, event | category | flops | bytes accessed | tf_op | source)
XLA Modules:
  0.0 437.8 jit_solution(11218612947903077331)
XLA Ops:
  6.5 4.5 %stack.2 = bf16[16,64,3072]{2,1,0:T(8,128)(2,1)} broadcast(bf16[64,3072]{1,0:T(8,128)(2,1)} %param.13), dimensions={1,2} | broadcast | bytes 6684672 | tf_op jit(solution)/shard_map/stack | solution.py:87
  11.0 12.0 %all-to-all-start = ((bf16[16,64,3072]{2,1,0:T(8,128)(2,1)}), bf16[16,64,3072]{2,1,0:T(8,128)(2,1)}, u32[]{:S(2)}, u32[]{:S(2)}) async-start(bf16[16,64,3072]{2,1,0:T(8,128)(2,1)} %stack.2), calls=%async_computation | async-start | bytes 12582912 | tf_op jit(solution)/shard_map/all_to_all | solution.py:87
  24.0 147.4 %all-to-all-done = bf16[16,64,3072]{2,1,0:T(8,128)(2,1)} async-done(((bf16[16,64,3072]{2,1,0:T(8,128)(2,1)}), bf16[16,64,3072]{2,1,0:T(8,128)(2,1)}, u32[]{:S(2)}, u32[]{:S(2)}) %all-to-all-start) | async-done | bytes 6291488 | tf_op jit(solution)/shard_map/all_to_all | solution.py:87
  171.4 4.7 %convolution_convert_fusion = bf16[256,3072]{1,0:T(8,128)(2,1)S(1)} fusion(bf16[1024,3072]{1,0:T(8,128)(2,1)} %bitcast.4, bf16[256,1024]{1,0:T(8,128)(2,1)S(1)} %copy-done.1, f32[256]{0:T(256)S(1)} %add_rsqrt_fusion.1), kind=kOutput, calls=%fused_computation.40 | convolution fusion | flops 1612185600 | bytes 8389632 | tf_op jit(solution)/shard_map/dot_general | solution.py:73
  176.1 2.4 collective-permute-start
  178.5 2.9 collective-permute-start.1
  182.6 7.6 %collective-permute-done = bf16[256,2048]{1,0:T(8,128)(2,1)} collective-permute-done((bf16[256,2048]{1,0:T(8,128)(2,1)S(1)}, bf16[256,2048]{1,0:T(8,128)(2,1)}, u32[]{:S(2)}, u32[]{:S(2)}) %collective-permute-start) | collective-permute-done | bytes 1048608 | tf_op jit(solution)/shard_map/ppermute | solution.py:21
  190.2 4.5 %collective-permute-done.1 = bf16[256,2048]{1,0:T(8,128)(2,1)} collective-permute-done((bf16[256,2048]{1,0:T(8,128)(2,1)S(1)}, bf16[256,2048]{1,0:T(8,128)(2,1)}, u32[]{:S(2)}, u32[]{:S(2)}) %collective-permute-start.1) | collective-permute-done | bytes 1048608 | tf_op jit(solution)/shard_map/ppermute | solution.py:23
  194.7 1.7 pad_maximum_fusion
  196.7 1.6 copy.17
  198.3 1.6 copy.16
  199.9 47.4 %while.26 = (s32[]{:T(128)}, bf16[16,256,64]{1,2,0:T(8,128)(2,1)S(1)}, bf16[16,256,64]{1,2,0:T(8,128)(2,1)}, bf16[16,768,64]{1,2,0:T(8,128)(2,1)}, bf16[16,768,6...) while((s32[]{:T(128)}, ...), condition=%wide.region_4.5_spmd.clone, body=%wide.region_1.4_spmd.clone.sunk | while | flops 52723200 | bytes 2633565 | solution.py:68
  200.0 1.4 fusion.111
  203.0 1.4 fusion.111
  205.9 1.4 fusion.111
  208.9 1.4 fusion.111
  210.5 1.3 fusion.113
  211.8 1.4 fusion.111
  213.5 1.3 fusion.113
  214.8 1.4 fusion.111
  216.5 1.3 fusion.113
  217.8 1.4 fusion.111
  219.4 1.3 fusion.113
  220.7 1.4 fusion.111
  222.4 1.3 fusion.113
  223.7 1.4 fusion.111
  225.3 1.3 fusion.113
  226.6 1.4 fusion.111
  228.3 1.3 fusion.113
  229.6 1.4 fusion.111
  231.2 1.3 fusion.113
  232.5 1.4 fusion.111
  234.2 1.3 fusion.113
  235.5 1.4 fusion.111
  237.2 1.3 fusion.113
  238.5 1.4 fusion.111
  240.1 1.3 fusion.113
  241.4 1.4 fusion.111
  243.1 1.3 fusion.113
  244.4 1.4 fusion.111
  247.4 2.4 bitcast_reduce_fusion
  249.8 16.4 %all_gather.17 = bf16[128,1024]{1,0:T(8,128)(2,1)S(1)} all-gather(bf16[8,1024]{1,0:T(8,128)(2,1)S(1)} %multiply_convert_fusion.2), channel_id=1, replica_groups=mesh['doc'=32,'seq'=16] {'seq'}, dimensions={0}, use_global_device_ids=true | all-gather | bytes 278528 | tf_op jit(solution)/shard_map/all_gather | solution.py:100
  269.3 2.4 convolution_convert_fusion.1
  271.9 110.9 %all-reduce.2.cloned.1.call-done = bf16[128,1024]{1,0:T(8,128)(2,1)} async-done(((bf16[128,1024]{1,0:T(8,128)(2,1)}), bf16[128,1024]{1,0:T(8,128)(2,1)}) %all-reduce.2.cloned.1.call-update) | async-done | bytes 262160 | tf_op jit(solution)/shard_map/psum | solution.py:113
  386.4 16.9 %all_gather.18 = bf16[128,2048]{0,1:T(8,128)(2,1)S(1)} all-gather(bf16[128,128]{0,1:T(8,128)(2,1)S(1)} %pad_maximum_fusion.1), channel_id=1, replica_groups=mesh['doc'=32,'seq'=16] {'seq'}, dimensions={1}, use_global_device_ids=true | all-gather | bytes 557056 | tf_op jit(solution)/shard_map/all_gather | solution.py:123
  404.0 7.0 %while.25 = (s32[]{:T(128)}, bf16[16,256,64]{1,2,0:T(8,128)(2,1)S(1)}, bf16[16,256,64]{1,2,0:T(8,128)(2,1)S(1)}, bf16[16,128,64]{2,1,0:T(8,128)(2,1)S(1)}, bf16[16,128,64]{2,1,0:T(8,128)(2,1)S(1)}, /*index=5*/s32[]{:T(128)}) while((s32[]{:T(128)}, bf16[16,256,64]{1,2,0:T(8,128)(2,1)S(1)}, bf16[16,256,64]{1,2,0:T(8,128)(2,1)S(1)}, ...), condition=%wide.region_15.16_spmd, body=%wide.region_12.15_spmd.sunk | while | flops 8617474 | bytes 531525 | solution.py:68
  411.0 17.2 %all-gather.8.cloned.1.call-done = bf16[1024,1024]{1,0:T(8,128)(2,1)} async-done(((bf16[64,1024]{1,0:T(8,128)(2,1)}), bf16[1024,1024]{1,0:T(8,128)(2,1)}) %all-gather.8.cloned.1.call-update) | async-done | bytes 2097168 | tf_op jit(solution)/shard_map/all_gather | solution.py:132
  428.2 3.1 fusion.37
  (118 shorter events, 26.2 us)
Async XLA Ops:
  6.5 261.1 %copy-start = (bf16[64,1024]{1,0:T(8,128)(2,1)S(1)}, bf16[64,1024]{1,0:T(8,128)(2,1)}, u32[]{:S(2)}) copy-start(bf16[64,1024]{1,0:T(8,128)(2,1)} %param.16) | copy-start | bytes 393220
  11.0 12.7 %copy-start.1 = (bf16[256,1024]{1,0:T(8,128)(2,1)S(1)}, bf16[256,1024]{1,0:T(8,128)(2,1)}, u32[]{:S(2)}) copy-start(bf16[256,1024]{1,0:T(8,128)(2,1)} %param.12) | copy-start | bytes 1572868
  11.0 160.3 %all-to-all-start = ((bf16[16,64,3072]{2,1,0:T(8,128)(2,1)}), bf16[16,64,3072]{2,1,0:T(8,128)(2,1)}, u32[]{:S(2)}, u32[]{:S(2)}) async-start(bf16[16,64,3072]{2,1,0:T(8,128)(2,1)} %stack.2), calls=%async_computation | async-start | bytes 12582912 | tf_op jit(solution)/shard_map/all_to_all | solution.py:87
  23.0 224.3 %all-gather.4.cloned.1.call-start = ((), (), s32[]{:S(2)}) async-start(), calls=%async_computation.1 | async-start | bytes 2228224 | tf_op jit(solution)/shard_map/all_gather | solution.py:95
  23.7 245.6 %all-gather.6.cloned.1.call-start = ((), (), s32[]{:S(2)}) async-start(), calls=%async_computation.2 | async-start | bytes 2228224 | tf_op jit(solution)/shard_map/all_gather | solution.py:129
  176.1 14.1 %collective-permute-start = (bf16[256,2048]{1,0:T(8,128)(2,1)S(1)}, bf16[256,2048]{1,0:T(8,128)(2,1)}, u32[]{:S(2)}, u32[]{:S(2)}) collective-permute-start(bf16[256,2048]{1,0:T(8,128)(2,1)S(1)} %slice.45), channel_id=1, source_target_pairs={{0,1},{1,2},{2,3},{3,4},{4,5},{5,6},{6,7},{7,8},{8,9},{9,10},{10,1... | collective-permute-start | bytes 3145736 | tf_op jit(solution)/shard_map/ppermute | solution.py:21
  178.5 16.2 %collective-permute-start.1 = (bf16[256,2048]{1,0:T(8,128)(2,1)S(1)}, bf16[256,2048]{1,0:T(8,128)(2,1)}, u32[]{:S(2)}, u32[]{:S(2)}) collective-permute-start(bf16[256,2048]{1,0:T(8,128)(2,1)S(1)} %slice.45), channel_id=1, source_target_pairs={{1,0},{2,1},{3,2},{4,3},{5,4},{6,5},{7,6},{8,7},{9,8},{10,9},{11,1... | collective-permute-start | bytes 3145736 | tf_op jit(solution)/shard_map/ppermute | solution.py:23
  181.4 201.3 %all-reduce.2.cloned.1.call-start = ((), (), s32[]{:S(2)}) async-start(), calls=%async_computation.3 | async-start | bytes 524288 | tf_op jit(solution)/shard_map/psum | solution.py:113
  199.9 47.4 %copy-start.2 = (bf16[256,1024]{1,0:T(8,128)(2,1)S(1)}, bf16[256,1024]{1,0:T(8,128)(2,1)}, u32[]{:S(2)}) copy-start(bf16[256,1024]{1,0:T(8,128)(2,1)} %param.12) | copy-start | bytes 1572868
  247.4 19.0 %copy-start.3 = (bf16[1024,3,64]{0,2,1:T(8,128)(2,1)S(1)}, bf16[1024,3,64]{0,2,1:T(8,128)(2,1)}, u32[]{:S(2)}) copy-start(bf16[1024,3,64]{0,2,1:T(8,128)(2,1)} %param.15) | copy-start | bytes 1179652
  268.5 159.7 %all-gather.8.cloned.1.call-start = ((), (), s32[]{:S(2)}) async-start(), calls=%async_computation.4 | async-start | bytes 2228224 | tf_op jit(solution)/shard_map/all_gather | solution.py:132
  269.3 114.6 %copy-start.4 = (bf16[1024,2,64]{0,2,1:T(8,128)(2,1)S(1)}, bf16[1024,2,64]{0,2,1:T(8,128)(2,1)}, u32[]{:S(2)}) copy-start(bf16[1024,2,64]{0,2,1:T(8,128)(2,1)} %param.18) | copy-start | bytes 786436
Sparse Core Ops, SparseCore 0:
  25.9 73.6 all-gather.3
  181.6 44.1 all-gather.5
  268.7 114.0 all-reduce.1
  385.0 43.1 all-gather.7
